TPU v7x, 32 devices: a whole 2x2x4 slice. The times are simulated.
32 devices in a mesh: row: 4 (over z), col: 8 (over y, x, core).
Axes of the slice: x: 2, y: 2, z: 4, core: 2. Of those that a mesh axis runs over, the one named last changes fastest.
Arguments:
- state_start: bfloat16 [512, 2048], P('row', 'col'), may hold values from -360 to 360
- actions: int32 [512, 2], P('row'), may hold values from 0 to 17
- targets: bfloat16 [2, 512, 2048], P(None, 'row'), may hold values from -504 to 504
- w_in: bfloat16 [2048, 4096], P('row', 'col'), may hold values from -0.125 to 0.125
- w_out: bfloat16 [4096, 2048], P('col', 'row'), may hold values from -0.09375 to 0.09375
- action_embed: bfloat16 [18, 4096], P(None, 'col'), may hold values from -6 to 6
Outputs:
- grad_w_in: float32 [2048, 4096], P('row', 'col')
- grad_w_out: float32 [4096, 2048], P('col', 'row')
All inputs are finite; a program needn't handle non-finite values.
Results may differ from a plain program's by a relative error of at most 0.035.
Values may be sent and summed in bfloat16 or wider, within the bound.
A program may use at most 64 MiB of HBM per device.

v0:
```python
import jax
import jax.numpy as jnp
from jax import lax
from jax.sharding import PartitionSpec as P

EPS = 1e-06
LOSS_SCALE = 128.0


def silu_grad(pre_act):
    gate_val = jax.nn.sigmoid(pre_act)
    return gate_val * (1.0 + pre_act * (1.0 - gate_val))


def cosine_from(state_f, target_f, self_dot, cross_dot, target_dot):
    inv_state = lax.rsqrt(self_dot + EPS)
    inv_target = lax.rsqrt(target_dot + EPS)
    cosine = cross_dot * inv_state * inv_target
    return -LOSS_SCALE * (
        target_f * inv_state * inv_target - cosine * state_f * inv_state * inv_state
    )


def shared_cosine(state, target):
    state_f = state.astype(jnp.float32)
    target_f = target.astype(jnp.float32)
    self_dot, cross_dot, target_dot = lax.psum(
        (
            jnp.sum(state_f * state_f, axis=-1),
            jnp.sum(state_f * target_f, axis=-1),
            jnp.sum(target_f * target_f, axis=-1),
        ),
        "col",
    )
    return cosine_from(
        state_f, target_f, self_dot[:, None], cross_dot[:, None], target_dot[:, None]
    )


def on_device(state_start, actions, targets, w_in, w_out, action_embed):
    unroll_steps = targets.shape[0]
    col_width = state_start.shape[1]
    w_in_panel = lax.all_gather(w_in, "row", axis=0, tiled=True)
    w_out_panel = lax.all_gather(w_out, "row", axis=1, tiled=True)
    col_start = lax.axis_index("col") * col_width
    action_ids = jnp.arange(action_embed.shape[0], dtype=jnp.int32)
    contract_last = (((1,), (1,)), ((), ()))
    current = state_start
    full_states = []
    pre_list = []
    hidden_list = []
    cos_terms = []
    for unroll in range(unroll_steps):
        full_rows = lax.all_gather(current, "col", axis=1, tiled=True)
        onehot = (actions[:, unroll][:, None] == action_ids[None, :]).astype(jnp.bfloat16)
        pre_act = jnp.dot(full_rows, w_in_panel, preferred_element_type=jnp.float32) + jnp.dot(
            onehot, action_embed, preferred_element_type=jnp.float32
        )
        hidden = jax.nn.silu(pre_act).astype(jnp.bfloat16)
        partial_value = jnp.dot(hidden, w_out_panel, preferred_element_type=jnp.float32)
        target = targets[unroll]
        branch = lax.psum_scatter(
            partial_value.astype(jnp.bfloat16), "col", scatter_dimension=1, tiled=True
        ).astype(jnp.float32)
        current = (current.astype(jnp.float32) + branch).astype(jnp.bfloat16)
        target_slice = lax.dynamic_slice_in_dim(target, col_start, col_width, 1)
        cos_terms.append(shared_cosine(current, target_slice))
        full_states.append(full_rows)
        pre_list.append(pre_act)
        hidden_list.append(hidden)
    state_grad = cos_terms[unroll_steps - 1].astype(jnp.bfloat16)
    grad_list = [None] * unroll_steps
    hid_grads = [None] * unroll_steps
    for unroll in reversed(range(unroll_steps)):
        grad_rows = lax.all_gather(state_grad, "col", axis=1, tiled=True)
        back = lax.dot_general(
            grad_rows, w_out_panel, contract_last, preferred_element_type=jnp.float32
        )
        hid_grad = (back * silu_grad(pre_list[unroll])).astype(jnp.bfloat16)
        grad_list[unroll] = grad_rows
        hid_grads[unroll] = hid_grad
        if unroll > 0:
            input_part = lax.dot_general(
                hid_grad, w_in_panel, contract_last, preferred_element_type=jnp.float32
            )
            summed = lax.psum_scatter(
                input_part.astype(jnp.bfloat16), "col", scatter_dimension=1, tiled=True
            ).astype(jnp.float32)
            state_grad = (state_grad.astype(jnp.float32) + summed + cos_terms[unroll - 1]).astype(
                jnp.bfloat16
            )
    grad_stack = jnp.stack(grad_list)
    hidden_stack = jnp.stack(hidden_list)
    state_stack = jnp.stack(full_states)
    hid_stack = jnp.stack(hid_grads)
    grad_feature_blocks = lax.all_to_all(grad_stack, "row", split_axis=2, concat_axis=1, tiled=True)
    hidden_all = lax.all_gather(hidden_stack, "row", axis=1, tiled=True)
    grad_w_out = jnp.einsum(
        "kbf,kbd->fd", hidden_all, grad_feature_blocks, preferred_element_type=jnp.float32
    )
    state_feature_blocks = lax.all_to_all(
        state_stack, "row", split_axis=2, concat_axis=1, tiled=True
    )
    hid_all = lax.all_gather(hid_stack, "row", axis=1, tiled=True)
    grad_w_in = jnp.einsum(
        "kbd,kbf->df", state_feature_blocks, hid_all, preferred_element_type=jnp.float32
    )
    return (grad_w_in, grad_w_out)


def solution(mesh):
    in_specs = (
        P("row", "col"),
        P("row", None),
        P(None, "row", None),
        P("row", "col"),
        P("col", "row"),
        P(None, "col"),
    )
    out_specs = (P("row", "col"), P("col", "row"))
    return jax.shard_map(
        on_device, mesh=mesh, in_specs=in_specs, out_specs=out_specs, check_vma=False
    )
```

profile of v0, /device:TPU:0, one launch (start us, length us, event | category | flops | bytes accessed | tf_op | source)
XLA Modules:
  0.0 336.0 jit_solution(11510671725148091114)
XLA Ops:
  7.2 0.7 all-gather.5.cloned.1.call-update
  8.0 0.7 all-gather.7.cloned.1.call-update
  8.7 12.7 %all_gather.24 = bf16[128,2048]{1,0:T(8,128)(2,1)S(1)} all-gather(bf16[128,256]{1,0:T(8,128)(2,1)} %param.6), channel_id=1, replica_groups=mesh['row'=4,'col'=8] {'col'}, dimensions={1}, use_global_device_ids=true | all-gather | bytes 589824 | tf_op jit(solution)/shard_map/all_gather | solution.py:54
  21.4 0.8 slice_bitcast_fusion
  22.2 0.2 fusion.23
  22.4 35.6 %all-gather.5.cloned.1.call-done = bf16[2048,512]{1,0:T(8,128)(2,1)} async-done(((bf16[512,512]{1,0:T(8,128)(2,1)}), bf16[2048,512]{1,0:T(8,128)(2,1)}) %all-gather.5.cloned.1.call-update) | async-done | bytes 2097168 | tf_op jit(solution)/shard_map/all_gather | solution.py:43
  58.0 2.0 convolution_add_fusion.1
  60.0 44.0 %all-gather.7.cloned.1.call-done = bf16[512,2048]{1,0:T(8,128)(2,1)} async-done(((bf16[512,512]{1,0:T(8,128)(2,1)}), bf16[512,2048]{1,0:T(8,128)(2,1)}) %all-gather.7.cloned.1.call-update) | async-done | bytes 2097168 | tf_op jit(solution)/shard_map/all_gather | solution.py:44
  104.0 2.9 convolution_convert_fusion.2
  106.9 0.0 reduce-scatter.6.cloned.1.call-start
  107.0 1.0 fusion.24
  107.9 2.1 fusion.29
  110.0 30.6 %reduce-scatter.4.cloned.1.call-done = bf16[128,256]{1,0:T(8,128)(2,1)} async-done(((bf16[128,2048]{1,0:T(8,128)(2,1)}), bf16[128,256]{1,0:T(8,128)(2,1)}) %reduce-scatter.4.cloned.1.call-update) | async-done | bytes 65552 | tf_op jit(solution)/shard_map/reduce_scatter | solution.py:62
  140.6 1.1 fusion.17
  141.8 10.9 %all_gather.27 = bf16[128,2048]{1,0:T(8,128)(2,1)S(1)} all-gather(bf16[128,256]{1,0:T(8,128)(2,1)S(1)} %get-tuple-element.14), channel_id=1, replica_groups=mesh['row'=4,'col'=8] {'col'}, dimensions={1}, use_global_device_ids=true | all-gather | bytes 589824 | tf_op jit(solution)/shard_map/all_gather | solution.py:54
  152.7 2.1 convolution_add_fusion
  154.8 2.2 convolution_convert_fusion.1
  157.1 34.2 %reduce-scatter.6.cloned.1.call-done = bf16[128,256]{1,0:T(8,128)(2,1)} async-done(((bf16[128,2048]{1,0:T(8,128)(2,1)}), bf16[128,256]{1,0:T(8,128)(2,1)}) %reduce-scatter.6.cloned.1.call-update) | async-done | bytes 65552 | tf_op jit(solution)/shard_map/reduce_scatter | solution.py:62
  191.3 1.0 fusion.10
  192.3 12.1 %all-reduce = (f32[128]{0:T(128)S(1)}, f32[128]{0:T(128)S(1)}, f32[128]{0:T(128)S(1)}, f32[128]{0:T(128)S(1)}, f32[128]{0:T(128)S(1)}, /*index=5*/f32[128]{0:T(128)S(1)}) all-reduce(f32[128]{0:T(128)S(1)} %get-tuple-element.5, f32[128]{0:T(128)S(1)} %get-tuple-element.6, ...), channel_id=1, replica_groups=mesh['row'=4,'col'=8] {'col'}, use_global_device_ids=true, to_apply=%region_7.8 | all-reduce | flops 768 | bytes 6144 | tf_op jit(solution)/shard_map/psum | solution.py:27
  204.5 1.0 fusion.8
  205.5 0.6 copy-done.5
  206.1 10.9 %all_gather.28 = bf16[128,2048]{1,0:T(8,128)(2,1)S(1)} all-gather(bf16[128,256]{1,0:T(8,128)(2,1)S(1)} %fusion.8), channel_id=1, replica_groups=mesh['row'=4,'col'=8] {'col'}, dimensions={1}, use_global_device_ids=true | all-gather | bytes 589824 | tf_op jit(solution)/shard_map/all_gather | solution.py:75
  217.0 0.8 copy-done.2
  217.8 2.4 fusion
  220.2 0.6 copy-done.7
  220.9 1.6 convolution_convert_fusion
  222.5 0.1 pad_maximum_fusion
  222.6 2.0 copy.11
  224.6 4.9 %all-to-all-start = ((bf16[2,128,2048]{1,0,2:T(2,128)(2,1)}), bf16[2,128,2048]{1,0,2:T(2,128)(2,1)S(1)}, u32[]{:S(2)}, u32[]{:S(2)}) async-start(bf16[2,128,2048]{1,0,2:T(2,128)(2,1)} %copy.11), calls=%async_computation.1 | async-start | bytes 2097152 | tf_op jit(solution)/shard_map/all_to_all | solution.py:101
  229.5 0.1 fusion.27
  229.6 1.0 fusion.28
  230.6 0.7 pad_maximum_fusion.3
  231.4 25.5 %reduce-scatter.8.cloned.1.call-done = bf16[128,256]{1,0:T(8,128)(2,1)} async-done(((bf16[128,2048]{1,0:T(8,128)(2,1)}), bf16[128,256]{1,0:T(8,128)(2,1)}) %reduce-scatter.8.cloned.1.call-update) | async-done | bytes 65552 | tf_op jit(solution)/shard_map/reduce_scatter | solution.py:86
  256.9 1.0 fusion.16
  258.0 10.9 %all_gather.29 = bf16[128,2048]{1,0:T(8,128)(2,1)S(1)} all-gather(bf16[128,256]{1,0:T(8,128)(2,1)S(1)} %fusion.16), channel_id=1, replica_groups=mesh['row'=4,'col'=8] {'col'}, dimensions={1}, use_global_device_ids=true | all-gather | bytes 589824 | tf_op jit(solution)/shard_map/all_gather | solution.py:75
  268.9 0.1 pad_maximum_fusion.1
  269.0 2.0 copy.13
  271.0 4.6 %all-to-all-start.1 = ((bf16[2,128,2048]{1,0,2:T(2,128)(2,1)}), bf16[2,128,2048]{1,0,2:T(2,128)(2,1)S(1)}, u32[]{:S(2)}, u32[]{:S(2)}) async-start(bf16[2,128,2048]{1,0,2:T(2,128)(2,1)} %copy.13), calls=%async_computation.4 | async-start | bytes 2097152 | tf_op jit(solution)/shard_map/all_to_all | solution.py:96
  275.6 2.5 fusion.2
  278.1 0.7 pad_maximum_fusion.2
  278.8 0.8 copy.18
  279.6 0.4 all_to_all.29
  280.1 33.4 %all-to-all-done.1 = bf16[2,128,2048]{1,0,2:T(2,128)(2,1)S(1)} async-done(((bf16[2,128,2048]{1,0,2:T(2,128)(2,1)}), bf16[2,128,2048]{1,0,2:T(2,128)(2,1)S(1)}, u32[]{:S(2)}, u32[]{:S(2)}) %all-to-all-start.1) | async-done | bytes 1048608 | tf_op jit(solution)/shard_map/all_to_all | solution.py:96
  313.5 0.8 copy.14
  314.3 2.9 convolution_bitcast_fusion
  317.2 9.0 %all-gather.9.cloned.1.call-done = bf16[2,512,512]{2,1,0:T(8,128)(2,1)} async-done(((bf16[2,128,512]{2,1,0:T(8,128)(2,1)}), bf16[2,512,512]{2,1,0:T(8,128)(2,1)}) %all-gather.9.cloned.1.call-update) | async-done | bytes 1048592 | tf_op jit(solution)/shard_map/all_gather | solution.py:104
  326.2 2.9 convolution_bitcast_fusion.1
  (32 shorter events, 0.3 us)
Async XLA Ops:
  7.2 15.0 %copy-start = (bf16[18,512]{1,0:T(8,128)(2,1)S(1)}, bf16[18,512]{1,0:T(8,128)(2,1)}, u32[]{:S(2)}) copy-start(bf16[18,512]{1,0:T(8,128)(2,1)} %param.11) | copy-start | bytes 55300
  7.2 50.8 %all-gather.5.cloned.1.call-start = ((), (), s32[]{:S(2)}) async-start(), calls=%async_computation.5 | async-start | bytes 2621440 | tf_op jit(solution)/shard_map/all_gather | solution.py:43
  7.9 96.1 %all-gather.7.cloned.1.call-start = ((), (), s32[]{:S(2)}) async-start(), calls=%async_computation.6 | async-start | bytes 2621440 | tf_op jit(solution)/shard_map/all_gather | solution.py:44
  8.7 132.0 %reduce-scatter.4.cloned.1.call-start = ((), (), s32[]{:S(2)}) async-start(), calls=%async_computation.7 | async-start | bytes 589824 | tf_op jit(solution)/shard_map/reduce_scatter | solution.py:62
  106.9 45.8 %copy-start.1 = (bf16[2048,512]{1,0:T(8,128)(2,1)S(1)}, bf16[2048,512]{1,0:T(8,128)(2,1)}, u32[]{:S(2)}) copy-start(bf16[2048,512]{1,0:T(8,128)(2,1)} %all-gather.5.cloned.1.call-done) | copy-start | bytes 6291460
  106.9 84.4 %reduce-scatter.6.cloned.1.call-start = ((), (), s32[]{:S(2)}) async-start(), calls=%async_computation.8 | async-start | bytes 589824 | tf_op jit(solution)/shard_map/reduce_scatter | solution.py:62
  110.0 31.7 %copy-start.4 = (bf16[1,128,2048]{2,1,0:T(8,128)(2,1)}, bf16[1,128,2048]{2,1,0:T(8,128)(2,1)S(1)}, u32[]{:S(2)}) copy-start(bf16[1,128,2048]{2,1,0:T(8,128)(2,1)S(1)} %get-tuple-element.16) | copy-start | bytes 1572868
  140.6 14.2 %copy-start.9 = (bf16[512,2048]{1,0:T(8,128)(2,1)S(1)}, bf16[512,2048]{1,0:T(8,128)(2,1)}, u32[]{:S(2)}) copy-start(bf16[512,2048]{1,0:T(8,128)(2,1)} %all-gather.7.cloned.1.call-done) | copy-start | bytes 6291460
  157.0 99.9 %reduce-scatter.8.cloned.1.call-start = ((), (), s32[]{:S(2)}) async-start(), calls=%async_computation.9 | async-start | bytes 589824 | tf_op jit(solution)/shard_map/reduce_scatter | solution.py:86
  205.5 0.6 copy-start.5
  217.0 0.8 copy-start.2
  220.2 0.6 copy-start.7
  224.6 32.3 %copy-start.6 = (bf16[128,256]{1,0:T(8,128)(2,1)S(1)}, bf16[128,256]{1,0:T(8,128)(2,1)}, u32[]{:S(2)}) copy-start(bf16[128,256]{1,0:T(8,128)(2,1)} %copy-done.5) | copy-start | bytes 196612
  224.6 44.2 %copy-start.3 = (bf16[128,2048]{1,0:T(8,128)(2,1)S(1)}, bf16[128,2048]{1,0:T(8,128)(2,1)}, u32[]{:S(2)}) copy-start(bf16[128,2048]{1,0:T(8,128)(2,1)} %copy-done.2) | copy-start | bytes 1572868
  224.6 46.3 %all-to-all-start = ((bf16[2,128,2048]{1,0,2:T(2,128)(2,1)}), bf16[2,128,2048]{1,0,2:T(2,128)(2,1)S(1)}, u32[]{:S(2)}, u32[]{:S(2)}) async-start(bf16[2,128,2048]{1,0,2:T(2,128)(2,1)} %copy.11), calls=%async_computation.1 | async-start | bytes 2097152 | tf_op jit(solution)/shard_map/all_to_all | solution.py:101
  229.5 84.8 %all-gather.11.cloned.1.call-start = ((), (), s32[]{:S(2)}) async-start(), calls=%async_computation.11 | async-start | bytes 1310720 | tf_op jit(solution)/shard_map/all_gather | solution.py:97
  271.0 42.5 %all-to-all-start.1 = ((bf16[2,128,2048]{1,0,2:T(2,128)(2,1)}), bf16[2,128,2048]{1,0,2:T(2,128)(2,1)S(1)}, u32[]{:S(2)}, u32[]{:S(2)}) async-start(bf16[2,128,2048]{1,0,2:T(2,128)(2,1)} %copy.13), calls=%async_computation.4 | async-start | bytes 2097152 | tf_op jit(solution)/shard_map/all_to_all | solution.py:96
  275.6 2.5 copy-start.8
  275.6 50.7 %all-gather.9.cloned.1.call-start = ((), (), s32[]{:S(2)}) async-start(), calls=%async_computation.10 | async-start | bytes 1310720 | tf_op jit(solution)/shard_map/all_gather | solution.py:104
Sparse Core Ops, SparseCore 0:
  9.6 48.3 all-gather.4
  59.5 44.4 all-gather.6
  107.7 32.8 reduce-scatter.3
  157.1 34.0 reduce-scatter.5
  222.6 34.2 reduce-scatter.7
  258.4 37.5 all-gather.10
  297.5 28.6 all-gather.8
where the time goes:
time: 337 us; the launch traced here: 336 us
  waiting for transfers between devices  214 us (64%)
  blocking collectives  57.5 us (17%)
  matrix products  22.8 us (7%)
  between operations  14.3 us (4%)
  local copies, waits for them, and re-layouts  11 us (3%)
  starting transfers between devices  9.7 us (3%)
  other arithmetic  6.97 us (2%)
    reduce_scatter x2, waiting for transfers between devices, on_device(): lax.psum_scatter(partial_value.astype(jnp.bfloat16), 'col', scatter_dimen...  64.8 us
    all_gather x1, waiting for transfers between devices, on_device(): w_out_panel = lax.all_gather(w_out, 'row', axis=1, tiled=True)  44 us
    all_gather x1, waiting for transfers between devices, on_device(): w_in_panel = lax.all_gather(w_in, 'row', axis=0, tiled=True)  35.6 us
    all_to_all x1, waiting for transfers between devices, on_device(): lax.all_to_all(grad_stack, 'row', split_axis=2, concat_axis=1, tiled=True)  33.4 us
    reduce_scatter x1, waiting for transfers between devices, on_device(): lax.psum_scatter(input_part.astype(jnp.bfloat16), 'col', scatter_dimensio...  25.5 us
    all_gather x2, blocking collectives, on_device(): full_rows = lax.all_gather(current, 'col', axis=1, tiled=True)  23.6 us
    all_gather x2, blocking collectives, on_device(): grad_rows = lax.all_gather(state_grad, 'col', axis=1, tiled=True)  21.8 us
    psum x1, blocking collectives, shared_cosine(): lax.psum((jnp.sum(state_f * state_f, axis=-1), jnp.sum(state_f * target_f...  12.1 us
  transfers between devices with their start and end apart: 9, of which 7 were waited for; matrix products, arithmetic and copies ran while one was open for 6% of the time, Pallas kernels for 0%

commit v1 on v0

--- a/solution.py
+++ b/solution.py
@@ -5,6 +5,18 @@
 
 EPS = 1e-06
 LOSS_SCALE = 128.0
+
+
+def doubled_up(value, axis, dim):
+    ways, here = (lax.axis_size(axis), lax.axis_index(axis))
+    grown, reach = (value, 1)
+    while reach < ways:
+        theirs = lax.ppermute(grown, axis, [(d, d ^ reach) for d in range(ways)])
+        mine_first = jnp.concatenate([grown, theirs], axis=dim)
+        theirs_first = jnp.concatenate([theirs, grown], axis=dim)
+        grown = jnp.where(here & reach == 0, mine_first, theirs_first)
+        reach = 2 * reach
+    return grown
 
 
 def silu_grad(pre_act):
@@ -51,7 +63,7 @@
     hidden_list = []
     cos_terms = []
     for unroll in range(unroll_steps):
-        full_rows = lax.all_gather(current, "col", axis=1, tiled=True)
+        full_rows = doubled_up(current, "col", 1)
         onehot = (actions[:, unroll][:, None] == action_ids[None, :]).astype(jnp.bfloat16)
         pre_act = jnp.dot(full_rows, w_in_panel, preferred_element_type=jnp.float32) + jnp.dot(
             onehot, action_embed, preferred_element_type=jnp.float32

time: 337 us -> 336 us (level)
  blocking collectives: 57.5 us -> 33.9 us
  waiting for transfers between devices: 214 us -> 231 us
  starting transfers between devices: 9.7 us -> 18 us
  matrix products: 22.8 us -> 19.4 us
    all_gather x2 -> x0, blocking collectives: 23.6 us -> none  [on_device(): full_rows = lax.all_gather(current, 'col', axis=1, tiled=True)]
    ppermute x0 -> x6, waiting for transfers between devices: none -> 21.1 us  [doubled_up(): theirs = lax.ppermute(grown, axis, [(d, d ^ reach) for d in range(ways)])]
    ppermute x0 -> x6, starting transfers between devices: none -> 8.42 us  [doubled_up(): theirs = lax.ppermute(grown, axis, [(d, d ^ reach) for d in range(ways)])]
    all_gather x1, waiting for transfers between devices: 35.6 us -> 32 us  [on_device(): w_in_panel = lax.all_gather(w_in, 'row', axis=0, tiled=True)]
  transfers between devices with their start and end apart: 9 -> 15, of which waited for: 7 -> 13; matrix products, arithmetic and copies ran while one was open for 6% -> 7% of each run, Pallas kernels for 0% -> 0%
where the time goes in v1:
time: 336 us; the launch traced here: 335 us
  waiting for transfers between devices  231 us (69%)
  blocking collectives  33.9 us (10%)
  matrix products  19.4 us (6%)
  starting transfers between devices  18 us (5%)
  between operations  14.4 us (4%)
  other arithmetic  10.2 us (3%)
  local copies, waits for them, and re-layouts  8.82 us (3%)
    reduce_scatter x2, waiting for transfers between devices, on_device(): lax.psum_scatter(partial_value.astype(jnp.bfloat16), 'col', scatter_dimen...  64.1 us
    all_gather x1, waiting for transfers between devices, on_device(): w_out_panel = lax.all_gather(w_out, 'row', axis=1, tiled=True)  44 us
    all_to_all x1, waiting for transfers between devices, on_device(): lax.all_to_all(grad_stack, 'row', split_axis=2, concat_axis=1, tiled=True)  33.5 us
    all_gather x1, waiting for transfers between devices, on_device(): w_in_panel = lax.all_gather(w_in, 'row', axis=0, tiled=True)  32 us
    reduce_scatter x1, waiting for transfers between devices, on_device(): lax.psum_scatter(input_part.astype(jnp.bfloat16), 'col', scatter_dimensio...  25.6 us
    all_gather x2, blocking collectives, on_device(): grad_rows = lax.all_gather(state_grad, 'col', axis=1, tiled=True)  21.8 us
    ppermute x6, waiting for transfers between devices, doubled_up(): theirs = lax.ppermute(grown, axis, [(d, d ^ reach) for d in range(ways)])  21.1 us
    psum x1, blocking collectives, shared_cosine(): lax.psum((jnp.sum(state_f * state_f, axis=-1), jnp.sum(state_f * target_f...  12.2 us
  transfers between devices with their start and end apart: 15, of which 13 were waited for; matrix products, arithmetic and copies ran while one was open for 7% of the time, Pallas kernels for 0%

profile of v1, /device:TPU:0, one launch (start us, length us, event | category | flops | bytes accessed | tf_op | source)
XLA Modules:
  0.0 335.3 jit_solution(4647112681859282861)
XLA Ops:
  7.2 0.7 all-gather.5.cloned.1.call-update
  8.0 0.7 all-gather.7.cloned.1.call-update
  9.3 1.1 collective-permute-done
  10.4 0.9 maximum_select_fusion.8
  11.3 2.9 collective-permute-start.1
  14.2 3.8 %collective-permute-done.1 = bf16[128,512]{1,0:T(8,128)(2,1)S(1)} collective-permute-done((bf16[128,512]{1,0:T(8,128)(2,1)S(1)}, bf16[128,512]{1,0:T(8,128)(2,1)S(1)}, u32[]{:S(2)}, u32[]{:S(2)}) %collective-permute-start.1) | collective-permute-done | bytes 131104 | tf_op jit(solution)/shard_map/ppermute | solution.py:14
  18.1 1.8 collective-permute-start.2
  20.0 0.8 slice_bitcast_fusion
  21.0 5.0 %collective-permute-done.2 = bf16[128,1024]{1,0:T(8,128)(2,1)S(1)} collective-permute-done((bf16[128,1024]{1,0:T(8,128)(2,1)S(1)}, bf16[128,1024]{1,0:T(8,128)(2,1)S(1)}, u32[]{:S(2)}, u32[]{:S(2)}) %collective-permute-start.2) | collective-permute-done | bytes 262176 | tf_op jit(solution)/shard_map/ppermute | solution.py:14
  26.0 32.0 %all-gather.5.cloned.1.call-done = bf16[2048,512]{1,0:T(8,128)(2,1)} async-done(((bf16[512,512]{1,0:T(8,128)(2,1)}), bf16[2048,512]{1,0:T(8,128)(2,1)}) %all-gather.5.cloned.1.call-update) | async-done | bytes 2097168 | tf_op jit(solution)/shard_map/all_gather | solution.py:55
  58.0 2.0 convolution_add_fusion.1
  60.0 44.0 %all-gather.7.cloned.1.call-done = bf16[512,2048]{1,0:T(8,128)(2,1)} async-done(((bf16[512,512]{1,0:T(8,128)(2,1)}), bf16[512,2048]{1,0:T(8,128)(2,1)}) %all-gather.7.cloned.1.call-update) | async-done | bytes 2097168 | tf_op jit(solution)/shard_map/all_gather | solution.py:56
  104.0 2.9 convolution_convert_fusion.2
  107.0 1.0 fusion.43
  108.0 32.0 %reduce-scatter.4.cloned.1.call-done = bf16[128,256]{1,0:T(8,128)(2,1)} async-done(((bf16[128,2048]{1,0:T(8,128)(2,1)}), bf16[128,256]{1,0:T(8,128)(2,1)}) %reduce-scatter.4.cloned.1.call-update) | async-done | bytes 65552 | tf_op jit(solution)/shard_map/reduce_scatter | solution.py:74
  140.1 1.0 fusion.29
  141.1 1.2 collective-permute-done.3
  142.4 1.5 collective-permute-start.4
  144.0 4.1 %collective-permute-done.4 = bf16[128,512]{1,0:T(8,128)(2,1)S(1)} collective-permute-done((bf16[128,512]{1,0:T(8,128)(2,1)S(1)}, bf16[128,512]{1,0:T(8,128)(2,1)S(1)}, u32[]{:S(2)}, u32[]{:S(2)}) %collective-permute-start.4) | collective-permute-done | bytes 131104 | tf_op jit(solution)/shard_map/ppermute | solution.py:14
  148.1 1.5 collective-permute-start.5
  149.9 5.8 %collective-permute-done.5 = bf16[128,1024]{1,0:T(8,128)(2,1)S(1)} collective-permute-done((bf16[128,1024]{1,0:T(8,128)(2,1)S(1)}, bf16[128,1024]{1,0:T(8,128)(2,1)S(1)}, u32[]{:S(2)}, u32[]{:S(2)}) %collective-permute-start.5) | collective-permute-done | bytes 262176 | tf_op jit(solution)/shard_map/ppermute | solution.py:14
  156.4 0.7 copy-done.6
  157.1 1.3 convolution_convert_fusion.1
  158.6 2.0 maximum_select_fusion.3
  160.6 32.1 %reduce-scatter.6.cloned.1.call-done = bf16[128,256]{1,0:T(8,128)(2,1)} async-done(((bf16[128,2048]{1,0:T(8,128)(2,1)}), bf16[128,256]{1,0:T(8,128)(2,1)}) %reduce-scatter.6.cloned.1.call-update) | async-done | bytes 65552 | tf_op jit(solution)/shard_map/reduce_scatter | solution.py:74
  192.7 1.0 fusion.22
  193.7 12.2 %all-reduce = (f32[128]{0:T(128)S(1)}, f32[128]{0:T(128)S(1)}, f32[128]{0:T(128)S(1)}, f32[128]{0:T(128)S(1)}, f32[128]{0:T(128)S(1)}, /*index=5*/f32[128]{0:T(128)S(1)}) all-reduce(f32[128]{0:T(128)S(1)} %get-tuple-element.5, f32[128]{0:T(128)S(1)} %get-tuple-element.6, ...), channel_id=1, replica_groups=mesh['row'=4,'col'=8] {'col'}, use_global_device_ids=true, to_apply=%region_7.8 | all-reduce | flops 768 | bytes 6144 | tf_op jit(solution)/shard_map/psum | solution.py:39
  205.9 1.0 fusion.20
  206.9 10.9 %all_gather.20 = bf16[128,2048]{1,0:T(8,128)(2,1)S(1)} all-gather(bf16[128,256]{1,0:T(8,128)(2,1)S(1)} %fusion.20), channel_id=1, replica_groups=mesh['row'=4,'col'=8] {'col'}, dimensions={1}, use_global_device_ids=true | all-gather | bytes 589824 | tf_op jit(solution)/shard_map/all_gather | solution.py:87
  217.8 2.4 fusion
  220.2 1.6 convolution_convert_fusion
  221.8 1.1 pad_maximum_fusion
  223.0 2.0 copy.11
  225.0 4.8 %all-to-all-start = ((bf16[2,128,2048]{1,0,2:T(2,128)(2,1)}), bf16[2,128,2048]{1,0,2:T(2,128)(2,1)S(1)}, u32[]{:S(2)}, u32[]{:S(2)}) async-start(bf16[2,128,2048]{1,0,2:T(2,128)(2,1)} %copy.11), calls=%async_computation.1 | async-start | bytes 2097152 | tf_op jit(solution)/shard_map/all_to_all | solution.py:113
  229.9 0.7 pad_maximum_fusion.3
  230.7 25.6 %reduce-scatter.8.cloned.1.call-done = bf16[128,256]{1,0:T(8,128)(2,1)} async-done(((bf16[128,2048]{1,0:T(8,128)(2,1)}), bf16[128,256]{1,0:T(8,128)(2,1)}) %reduce-scatter.8.cloned.1.call-update) | async-done | bytes 65552 | tf_op jit(solution)/shard_map/reduce_scatter | solution.py:98
  256.3 1.0 fusion.28
  257.3 10.9 %all_gather.21 = bf16[128,2048]{1,0:T(8,128)(2,1)S(1)} all-gather(bf16[128,256]{1,0:T(8,128)(2,1)S(1)} %fusion.28), channel_id=1, replica_groups=mesh['row'=4,'col'=8] {'col'}, dimensions={1}, use_global_device_ids=true | all-gather | bytes 589824 | tf_op jit(solution)/shard_map/all_gather | solution.py:87
  268.3 2.0 copy.13
  270.3 4.6 %all-to-all-start.1 = ((bf16[2,128,2048]{1,0,2:T(2,128)(2,1)}), bf16[2,128,2048]{1,0,2:T(2,128)(2,1)S(1)}, u32[]{:S(2)}, u32[]{:S(2)}) async-start(bf16[2,128,2048]{1,0,2:T(2,128)(2,1)} %copy.13), calls=%async_computation.4 | async-start | bytes 2097152 | tf_op jit(solution)/shard_map/all_to_all | solution.py:108
  274.9 2.4 fusion.2
  277.3 0.7 pad_maximum_fusion.2
  278.1 0.8 copy.18
  279.4 33.5 %all-to-all-done.1 = bf16[2,128,2048]{1,0,2:T(2,128)(2,1)S(1)} async-done(((bf16[2,128,2048]{1,0,2:T(2,128)(2,1)}), bf16[2,128,2048]{1,0,2:T(2,128)(2,1)S(1)}, u32[]{:S(2)}, u32[]{:S(2)}) %all-to-all-start.1) | async-done | bytes 1048608 | tf_op jit(solution)/shard_map/all_to_all | solution.py:108
  312.8 0.8 copy.14
  313.7 2.9 convolution_bitcast_fusion
  316.6 9.0 %all-gather.9.cloned.1.call-done = bf16[2,512,512]{2,1,0:T(8,128)(2,1)} async-done(((bf16[2,128,512]{2,1,0:T(8,128)(2,1)}), bf16[2,512,512]{2,1,0:T(8,128)(2,1)}) %all-gather.9.cloned.1.call-update) | async-done | bytes 1048592 | tf_op jit(solution)/shard_map/all_gather | solution.py:116
  325.5 2.9 convolution_bitcast_fusion.1
  (52 shorter events, 3.2 us)
Async XLA Ops:
  7.2 13.6 %copy-start = (bf16[18,512]{1,0:T(8,128)(2,1)S(1)}, bf16[18,512]{1,0:T(8,128)(2,1)}, u32[]{:S(2)}) copy-start(bf16[18,512]{1,0:T(8,128)(2,1)} %param.11) | copy-start | bytes 55300
  7.2 50.8 %all-gather.5.cloned.1.call-start = ((), (), s32[]{:S(2)}) async-start(), calls=%async_computation.5 | async-start | bytes 2621440 | tf_op jit(solution)/shard_map/all_gather | solution.py:55
  7.9 96.1 %all-gather.7.cloned.1.call-start = ((), (), s32[]{:S(2)}) async-start(), calls=%async_computation.6 | async-start | bytes 2621440 | tf_op jit(solution)/shard_map/all_gather | solution.py:56
  8.7 131.4 %reduce-scatter.4.cloned.1.call-start = ((), (), s32[]{:S(2)}) async-start(), calls=%async_computation.7 | async-start | bytes 589824 | tf_op jit(solution)/shard_map/reduce_scatter | solution.py:74
  8.7 1.7 collective-permute-start
  11.3 6.7 %collective-permute-start.1 = (bf16[128,512]{1,0:T(8,128)(2,1)S(1)}, bf16[128,512]{1,0:T(8,128)(2,1)S(1)}, u32[]{:S(2)}, u32[]{:S(2)}) collective-permute-start(bf16[128,512]{1,0:T(8,128)(2,1)S(1)} %maximum_select_fusion.8), channel_id=1, source_target_pairs={{0,2},{1,3},{2,0},{3,1},{4,6},{5,7},{6,4},{7,5},{8,10},{9,11},{10,... | collective-permute-start | bytes 393224 | tf_op jit(solution)/shard_map/ppermute | solution.py:14
  18.1 7.9 %collective-permute-start.2 = (bf16[128,1024]{1,0:T(8,128)(2,1)S(1)}, bf16[128,1024]{1,0:T(8,128)(2,1)S(1)}, u32[]{:S(2)}, u32[]{:S(2)}) collective-permute-start(bf16[128,1024]{1,0:T(8,128)(2,1)S(1)} %maximum_select_fusion.6), channel_id=1, source_target_pairs={{0,4},{1,5},{2,6},{3,7},{4,0},{5,1},{6,2},{7,3},{8,12},{9,13},{10,... | collective-permute-start | bytes 786440 | tf_op jit(solution)/shard_map/ppermute | solution.py:14
  26.0 78.0 %copy-start.8 = (bf16[128,1024]{1,0:T(8,128)(2,1)}, bf16[128,1024]{1,0:T(8,128)(2,1)S(1)}, u32[]{:S(2)}) copy-start(bf16[128,1024]{1,0:T(8,128)(2,1)S(1)} %collective-permute-done.2) | copy-start | bytes 786436
  60.0 44.0 %copy-start.3 = (f32[128,512]{1,0:T(8,128)}, f32[128,512]{1,0:T(8,128)S(1)}, u32[]{:S(2)}) copy-start(f32[128,512]{1,0:T(8,128)S(1)} %convolution_add_fusion.1) | copy-start | bytes 786436
  60.0 47.0 %copy-start.2 = (bf16[2,128,2048]{2,1,0:T(8,128)(2,1)S(1)}, bf16[2,128,2048]{2,1,0:T(8,128)(2,1)}, u32[]{:S(2)}) copy-start(bf16[2,128,2048]{2,1,0:T(8,128)(2,1)} %param.8) | copy-start | bytes 3145732
  106.9 48.8 %copy-start.1 = (bf16[2048,512]{1,0:T(8,128)(2,1)S(1)}, bf16[2048,512]{1,0:T(8,128)(2,1)}, u32[]{:S(2)}) copy-start(bf16[2048,512]{1,0:T(8,128)(2,1)} %all-gather.5.cloned.1.call-done) | copy-start | bytes 6291460
  106.9 85.7 %reduce-scatter.6.cloned.1.call-start = ((), (), s32[]{:S(2)}) async-start(), calls=%async_computation.8 | async-start | bytes 589824 | tf_op jit(solution)/shard_map/reduce_scatter | solution.py:74
  141.1 1.3 collective-permute-start.3
  142.4 5.6 %collective-permute-start.4 = (bf16[128,512]{1,0:T(8,128)(2,1)S(1)}, bf16[128,512]{1,0:T(8,128)(2,1)S(1)}, u32[]{:S(2)}, u32[]{:S(2)}) collective-permute-start(bf16[128,512]{1,0:T(8,128)(2,1)S(1)} %maximum_select_fusion.9), channel_id=1, source_target_pairs={{0,2},{1,3},{2,0},{3,1},{4,6},{5,7},{6,4},{7,5},{8,10},{9,11},{10,... | collective-permute-start | bytes 393224 | tf_op jit(solution)/shard_map/ppermute | solution.py:14
  148.1 7.6 %collective-permute-start.5 = (bf16[128,1024]{1,0:T(8,128)(2,1)S(1)}, bf16[128,1024]{1,0:T(8,128)(2,1)S(1)}, u32[]{:S(2)}, u32[]{:S(2)}) collective-permute-start(bf16[128,1024]{1,0:T(8,128)(2,1)S(1)} %maximum_select_fusion.7), channel_id=1, source_target_pairs={{0,4},{1,5},{2,6},{3,7},{4,0},{5,1},{6,2},{7,3},{8,12},{9,13},{10,... | collective-permute-start | bytes 786440 | tf_op jit(solution)/shard_map/ppermute | solution.py:14
  149.9 7.2 %copy-start.11 = (bf16[512,2048]{1,0:T(8,128)(2,1)S(1)}, bf16[512,2048]{1,0:T(8,128)(2,1)}, u32[]{:S(2)}) copy-start(bf16[512,2048]{1,0:T(8,128)(2,1)} %all-gather.7.cloned.1.call-done) | copy-start | bytes 6291460
  155.7 0.7 copy-start.10
  156.4 0.7 copy-start.6
  157.1 1.3 copy-start.9
  158.4 97.9 %reduce-scatter.8.cloned.1.call-start = ((), (), s32[]{:S(2)}) async-start(), calls=%async_computation.9 | async-start | bytes 589824 | tf_op jit(solution)/shard_map/reduce_scatter | solution.py:98
  223.0 6.8 %copy-start.4 = (f32[128,512]{1,0:T(8,128)S(1)}, f32[128,512]{1,0:T(8,128)}, u32[]{:S(2)}) copy-start(f32[128,512]{1,0:T(8,128)} %copy-done.3) | copy-start | bytes 786436
  223.0 6.9 %copy-start.7 = (f32[128,512]{1,0:T(8,128)S(1)}, f32[128,512]{1,0:T(8,128)}, u32[]{:S(2)}) copy-start(f32[128,512]{1,0:T(8,128)} %copy-done.6) | copy-start | bytes 786436
  225.0 45.3 %all-to-all-start = ((bf16[2,128,2048]{1,0,2:T(2,128)(2,1)}), bf16[2,128,2048]{1,0,2:T(2,128)(2,1)S(1)}, u32[]{:S(2)}, u32[]{:S(2)}) async-start(bf16[2,128,2048]{1,0,2:T(2,128)(2,1)} %copy.11), calls=%async_computation.1 | async-start | bytes 2097152 | tf_op jit(solution)/shard_map/all_to_all | solution.py:113
  229.8 83.9 %all-gather.11.cloned.1.call-start = ((), (), s32[]{:S(2)}) async-start(), calls=%async_computation.11 | async-start | bytes 1310720 | tf_op jit(solution)/shard_map/all_gather | solution.py:109
  268.3 6.6 %copy-start.5 = (f32[128,512]{1,0:T(8,128)S(1)}, f32[128,512]{1,0:T(8,128)}, u32[]{:S(2)}) copy-start(f32[128,512]{1,0:T(8,128)} %copy-done.3) | copy-start | bytes 786436
  270.3 42.6 %all-to-all-start.1 = ((bf16[2,128,2048]{1,0,2:T(2,128)(2,1)}), bf16[2,128,2048]{1,0,2:T(2,128)(2,1)S(1)}, u32[]{:S(2)}, u32[]{:S(2)}) async-start(bf16[2,128,2048]{1,0,2:T(2,128)(2,1)} %copy.13), calls=%async_computation.4 | async-start | bytes 2097152 | tf_op jit(solution)/shard_map/all_to_all | solution.py:108
  274.9 50.7 %all-gather.9.cloned.1.call-start = ((), (), s32[]{:S(2)}) async-start(), calls=%async_computation.10 | async-start | bytes 1310720 | tf_op jit(solution)/shard_map/all_gather | solution.py:116
Sparse Core Ops, SparseCore 0:
  9.6 48.3 all-gather.4
  59.5 44.4 all-gather.6
  107.1 32.8 reduce-scatter.3
  158.5 34.0 reduce-scatter.5
  222.0 34.2 reduce-scatter.7
  257.7 37.5 all-gather.10
  296.8 28.6 all-gather.8
